TPU v7x, 512 devices: a whole 4x8x8 slice. The times are simulated.
512 devices in a mesh: seq: 32 (over x, y), dp: 8 (over z), domain: 2 (over core).
Axes of the slice: x: 4, y: 8, z: 8, core: 2. Of those that a mesh axis runs over, the one named last changes fastest.
Arguments:
- history: bfloat16 [2, 8, 8192, 1024], P('domain', 'dp', 'seq'), may hold values from -6 to 6
- qkv_weight: bfloat16 [2, 1024, 3072], P('domain', 'seq'), may hold values from -0.375 to 0.375
- norm_gain: float32 [2, 1024], P('domain'), may hold values from 0.1 to 1.9
- pool_gain: float32 [2, 1024], P('domain'), may hold values from 0.1 to 1.9
- lengths: int32 [2, 8], P('domain', 'dp'), may hold values from 1024 to 8192, as said below
- positives: int32 [8], replicated, may hold values from 0 to 7, each once
Outputs:
- user_vec: bfloat16 [2, 8, 1024], P('domain', 'dp', 'seq')
- loss: float32 [2, 8], P('domain', 'dp')
Inputs may be any that keep to these rules, and one draw needn't show every extreme that they name: `lengths`: in each domain one user has exactly 8192 valid events and another exactly 1024. `positives`: each user of the second domain is named exactly once.
All inputs are finite; a program needn't handle non-finite values.
Results may differ from a plain program's by a relative error of at most 0.0085.
Values may be sent and summed in bfloat16 or wider, within the bound.
A program may use at most 64 MiB of HBM per device.

v0:
```python
import jax
import jax.numpy as jnp
from jax import lax
from jax.sharding import PartitionSpec as P

HEADS = 8
HEAD_DIM = 128
logit_scale = 20.0
epsilon = 1e-06
highest = lax.Precision.HIGHEST


def carried_in(part, axis, combine, identity):
    place = lax.axis_index(axis)
    gathered = jax.tree.map(lambda a: lax.all_gather(a, axis), part)
    state = jax.tree.map(lambda a, e: jnp.zeros_like(a) + jnp.asarray(e, a.dtype), part, identity)

    def one(hop, state):
        return combine(
            state, jax.tree.map(lambda a: lax.dynamic_index_in_dim(a, hop, 0, False), gathered)
        )

    return lax.fori_loop(0, place, one, state)


def partner_2(block, axis, stride):
    count = lax.axis_size(axis)
    route = []
    for low in range(count):
        high = low | 1 << stride
        if high != low and high < count:
            route += [(low, high), (high, low)]
    return lax.ppermute(block, axis, route)


def feature_map(values):
    return jax.nn.elu(values) + 1.0


def add_pair(earlier, later):
    return (earlier[0] + later[0], earlier[1] + later[1])


def shards(history, qkv_weight, norm_gain, pool_gain, lengths, positives):
    seq_count = lax.axis_size("seq")
    seq_place = lax.axis_index("seq")
    group_place = lax.axis_index("dp")
    domain_place = lax.axis_index("domain")
    events = history[0]
    users_dev, tokens_dev, width = events.shape
    row_count = users_dev * tokens_dev
    wide = events.astype(jnp.float32)
    normed = (
        wide * lax.rsqrt(jnp.mean(wide * wide, -1, keepdims=True) + epsilon) * norm_gain[0]
    ).astype(jnp.bfloat16)
    normed = normed.reshape(row_count, width)
    rows_here = qkv_weight[0]

    def add_rows(piece):
        return jnp.dot(normed, piece, preferred_element_type=jnp.float32)

    query_raw = add_rows(lax.all_gather(rows_here[:, :width], "seq", axis=0, tiled=True))
    key_raw = add_rows(lax.all_gather(rows_here[:, width : 2 * width], "seq", axis=0, tiled=True))
    value_raw = add_rows(lax.all_gather(rows_here[:, 2 * width :], "seq", axis=0, tiled=True))
    positions = seq_place * tokens_dev + jnp.arange(tokens_dev)
    valid = positions[None, :] < lengths[0][:, None]
    shape_heads = (users_dev, tokens_dev, HEADS, HEAD_DIM)
    queries = feature_map(query_raw).astype(jnp.bfloat16).reshape(shape_heads)
    key_feats = (
        jnp.where(valid.reshape(row_count)[:, None], feature_map(key_raw), 0.0)
        .astype(jnp.bfloat16)
        .reshape(shape_heads)
    )
    val_feats = value_raw.astype(jnp.bfloat16).reshape(shape_heads)
    local_state = jnp.einsum(
        "uthc,uthd->uhcd", key_feats, val_feats, preferred_element_type=jnp.float32
    )
    local_total = jnp.sum(key_feats.astype(jnp.float32), axis=1)
    state_before, total_before = carried_in(
        (local_state, local_total),
        "seq",
        add_pair,
        (jnp.zeros_like(local_state), jnp.zeros_like(local_total)),
    )
    causal = jnp.arange(tokens_dev)[:, None] >= jnp.arange(tokens_dev)[None, :]
    scores = jnp.einsum("uthc,ushc->uhts", queries, key_feats, preferred_element_type=jnp.float32)
    scores = jnp.where(causal, scores, 0.0)
    denominator = jnp.sum(scores, axis=-1) + jnp.einsum(
        "uthc,uhc->uht", queries.astype(jnp.float32), total_before, precision=highest
    )
    numerator = jnp.einsum(
        "uhts,ushc->uthc",
        scores.astype(jnp.bfloat16),
        val_feats,
        preferred_element_type=jnp.float32,
    )
    numerator = numerator + jnp.einsum(
        "uthc,uhcd->uthd",
        queries,
        state_before.astype(jnp.bfloat16),
        preferred_element_type=jnp.float32,
    )
    attended = numerator / jnp.transpose(denominator, (0, 2, 1))[..., None]
    attended = attended.reshape(users_dev, tokens_dev, width)
    partial_value = jnp.sum(jnp.where(valid[..., None], wide + attended, 0.0), axis=1)
    piece_width = width // seq_count
    gain_row = pool_gain[0]
    pooled = lax.psum(partial_value, "seq")
    factor = lax.rsqrt(jnp.mean(pooled * pooled, -1, keepdims=True) + epsilon)
    full_vec = (pooled * factor * gain_row).astype(jnp.bfloat16)
    out_vec = lax.dynamic_slice_in_dim(full_vec, seq_place * piece_width, piece_width, 1)
    group = lax.all_gather(full_vec, "dp", axis=0, tiled=True)
    other = partner_2(group, "domain", 0)
    logits = jnp.einsum("uc,vc->uv", full_vec, other, preferred_element_type=jnp.float32) * (
        logit_scale / width
    )
    users_all = other.shape[0]
    own_index = group_place * users_dev + jnp.arange(users_dev)
    targets = lax.dynamic_slice_in_dim(positives, group_place * users_dev, users_dev)
    forward_pair = targets[:, None] == jnp.arange(users_all)[None, :]
    backward_pair = positives[None, :] == own_index[:, None]
    partner = jnp.where(domain_place == 0, forward_pair, backward_pair)
    loss = jnp.log(jnp.sum(jnp.exp(logits), axis=-1)) - jnp.sum(
        jnp.where(partner, logits, 0.0), axis=-1
    )
    return (out_vec[None], loss[None])


def solution(mesh):
    placed = (
        P("domain", "dp", "seq", None),
        P("domain", "seq", None),
        P("domain", None),
        P("domain", None),
        P("domain", "dp"),
        P(),
    )
    return jax.shard_map(
        shards,
        mesh=mesh,
        in_specs=placed,
        out_specs=(P("domain", "dp", "seq"), P("domain", "dp")),
        check_vma=False,
    )
```

profile of v0, /device:TPU:1, one launch (start us, length us, event | category | flops | bytes accessed | tf_op | source)
XLA Modules:
  0.0 566.4 jit_solution(12575679889314143297)
XLA Ops:
  7.2 0.0 all-gather.11.cloned.1.call-start
  7.2 1.6 fusion.51
  8.8 0.0 all-gather.11.cloned.1.call-update
  8.8 0.0 all-gather.7.cloned.1.call-start
  8.9 0.7 all-gather.7.cloned.1.call-update
  9.6 0.0 all-gather.9.cloned.1.call-start
  9.6 0.7 all-gather.9.cloned.1.call-update
  10.3 0.0 all-gather.13.cloned.1.call-start
  11.0 1.2 fusion.5
  12.2 82.9 %all-gather.11.cloned.1.call-done = bf16[1024,1024]{1,0:T(8,128)(2,1)} async-done(((bf16[32,1024]{1,0:T(8,128)(2,1)}), bf16[1024,1024]{1,0:T(8,128)(2,1)}) %all-gather.11.cloned.1.call-update) | async-done | bytes 2097168 | tf_op jit(solution)/shard_map/all_gather | solution.py:63
  95.1 0.0 copy-start
  95.1 0.0 copy-start.2
  95.1 3.0 convert_reduce_fusion
  98.1 0.2 copy.43
  98.3 0.0 copy-start.3
  98.3 80.6 %all-gather.7.cloned.1.call-done = bf16[1024,1024]{1,0:T(8,128)(2,1)} async-done(((bf16[32,1024]{1,0:T(8,128)(2,1)}), bf16[1024,1024]{1,0:T(8,128)(2,1)}) %all-gather.7.cloned.1.call-update) | async-done | bytes 2097168 | tf_op jit(solution)/shard_map/all_gather | solution.py:64
  178.9 0.0 copy-done
  178.9 0.0 copy-done.2
  178.9 2.4 fusion.3
  181.3 1.1 fusion.29
  182.4 0.0 all-gather.13.cloned.1.call-update
  182.4 0.0 copy-done.3
  182.4 0.7 dynamic_slice.15
  183.1 31.5 %all_gather.30 = f32[32,1,8,128]{3,2,1,0:T(8,128)S(1)} all-gather(f32[1,1,8,128]{3,2,1,0:T(8,128)S(1)} %bitcast.122), channel_id=1, replica_groups=mesh['seq'=32,'dp'=8,'domain'=2] {'seq'}, dimensions={0}, use_global_device_ids=true | all-gather | bytes 135168 | tf_op jit(solution)/shard_map/all_gather | solution.py:15
  214.6 48.1 %all-gather.9.cloned.1.call-done = bf16[1024,1024]{1,0:T(8,128)(2,1)} async-done(((bf16[32,1024]{1,0:T(8,128)(2,1)}), bf16[1024,1024]{1,0:T(8,128)(2,1)}) %all-gather.9.cloned.1.call-update) | async-done | bytes 2097168 | tf_op jit(solution)/shard_map/all_gather | solution.py:62
  262.7 2.7 fusion.22
  265.4 0.0 copy-start.4
  265.4 0.5 select_reduce_fusion
  266.0 0.4 fusion.11
  266.3 145.7 %all-gather.13.cloned.1.call-done = f32[256,128,128]{2,1,0:T(8,128)} async-done(((f32[8,128,128]{2,1,0:T(8,128)}), f32[256,128,128]{2,1,0:T(8,128)}) %all-gather.13.cloned.1.call-update) | async-done | bytes 16777232 | tf_op jit(solution)/shard_map/all_gather | solution.py:15
  412.1 0.0 copy-done.4
  412.1 0.5 fusion.24
  412.6 1.4 fusion.21
  414.0 0.0 copy-start.1
  414.0 0.3 copy.37
  414.3 0.2 fusion.7
  414.6 94.9 %psum.7 = f32[1,1024]{1,0:T(1,128)S(1)} all-reduce(f32[1,1024]{1,0:T(1,128)S(1)} %bitcast.119), channel_id=1, replica_groups=mesh['seq'=32,'dp'=8,'domain'=2] {'seq'}, use_global_device_ids=true, to_apply=%region_6.7 | all-reduce | flops 1024 | bytes 8192 | tf_op jit(solution)/shard_map/psum | solution.py:108
  509.5 0.6 multiply_reduce_fusion
  510.8 0.0 copy-done.1
  510.8 20.9 %all-gather.1 = bf16[8,1,1024]{2,1,0:T(2,128)(2,1)S(1)} all-gather(bf16[1,1,1024]{2,1,0:T(2,128)(2,1)S(1)} %bitcast.121), channel_id=1, replica_groups=mesh['seq'=32,'dp'=8,'domain'=2] {'dp'}, dimensions={0}, use_global_device_ids=true | all-gather | bytes 18432 | tf_op jit(solution)/shard_map/all_gather | solution.py:112
  531.7 23.3 %collective-permute-start = (bf16[8,1024]{1,0:T(8,128)(2,1)S(1)}, bf16[8,1024]{1,0:T(8,128)(2,1)S(1)}, u32[]{:S(2)}, u32[]{:S(2)}) collective-permute-start(bf16[8,1024]{1,0:T(8,128)(2,1)S(1)} %bitcast.120), channel_id=1, source_target_pairs={{0,1},{1,0},{2,3},{3,2},{4,5},{5,4},{6,7},{7,6},{8,9},{9,8},{10,11... | collective-permute-start | bytes 49160 | tf_op jit(solution)/shard_map/ppermute | solution.py:33
  555.0 0.6 dynamic-slice_bitcast_fusion
  555.6 0.2 collective-permute-done
  555.8 1.5 fusion.40
  (9 shorter events, 0.1 us)
Async XLA Ops:
  7.2 87.9 %all-gather.11.cloned.1.call-start = ((), (), s32[]{:S(2)}) async-start(), calls=%async_computation.2 | async-start | bytes 2162688 | tf_op jit(solution)/shard_map/all_gather | solution.py:63
  8.8 170.1 %all-gather.7.cloned.1.call-start = ((), (), s32[]{:S(2)}) async-start(), calls=%async_computation | async-start | bytes 2162688 | tf_op jit(solution)/shard_map/all_gather | solution.py:64
  9.6 253.1 %all-gather.9.cloned.1.call-start = ((), (), s32[]{:S(2)}) async-start(), calls=%async_computation.1 | async-start | bytes 2162688 | tf_op jit(solution)/shard_map/all_gather | solution.py:62
  10.3 401.7 %all-gather.13.cloned.1.call-start = ((), (), s32[]{:S(2)}) async-start(), calls=%async_computation.3 | async-start | bytes 17301504 | tf_op jit(solution)/shard_map/all_gather | solution.py:15
  95.1 83.8 %copy-start = (bf16[1,1,256,1024]{3,2,1,0:T(8,128)(2,1)S(1)}, bf16[1,1,256,1024]{3,2,1,0:T(8,128)(2,1)}, u32[]{:S(2)}) copy-start(bf16[1,1,256,1024]{3,2,1,0:T(8,128)(2,1)} %param.8) | copy-start | bytes 1572868
  95.1 83.8 %copy-start.2 = (f32[1,1024]{1,0:T(1,128)S(1)}, f32[1,1024]{1,0:T(1,128)}, u32[]{:S(2)}) copy-start(f32[1,1024]{1,0:T(1,128)} %param.10) | copy-start | bytes 12292
  98.3 84.1 %copy-start.3 = (s32[8]{0:T(128)S(1)}, s32[8]{0:T(128)}, u32[]{:S(2)}) copy-start(s32[8]{0:T(128)} %param.13) | copy-start | bytes 100
  265.4 146.6 %copy-start.4 = (bf16[32,8,8,128]{3,2,1,0:T(8,128)(2,1)}, bf16[32,8,8,128]{3,2,1,0:T(8,128)(2,1)S(1)}, u32[]{:S(2)}) copy-start(bf16[32,8,8,128]{3,2,1,0:T(8,128)(2,1)S(1)} %fusion.22) | copy-start | bytes 1572868
  414.0 96.8 %copy-start.1 = (f32[1,1024]{1,0:T(1,128)S(1)}, f32[1,1024]{1,0:T(1,128)}, u32[]{:S(2)}) copy-start(f32[1,1024]{1,0:T(1,128)} %param.11) | copy-start | bytes 12292
  531.7 24.1 %collective-permute-start = (bf16[8,1024]{1,0:T(8,128)(2,1)S(1)}, bf16[8,1024]{1,0:T(8,128)(2,1)S(1)}, u32[]{:S(2)}, u32[]{:S(2)}) collective-permute-start(bf16[8,1024]{1,0:T(8,128)(2,1)S(1)} %bitcast.120), channel_id=1, source_target_pairs={{0,1},{1,0},{2,3},{3,2},{4,5},{5,4},{6,7},{7,6},{8,9},{9,8},{10,11... | collective-permute-start | bytes 49160 | tf_op jit(solution)/shard_map/ppermute | solution.py:33
Sparse Core Ops, SparseCore 0:
  11.1 83.9 all-gather.10
  98.3 80.6 all-gather.6
  182.1 80.5 all-gather.8
  265.7 146.2 all-gather.12
where the time goes:
time: 568 us; the launch traced here: 566 us
  waiting for transfers between devices  359 us (63%)
  blocking collectives  147 us (26%)
  starting transfers between devices  23.4 us (4%)
  between operations  17.8 us (3%)
  matrix products  13.5 us (2%)
    all_gather x1, waiting for transfers between devices, carried_in(): gathered = jax.tree.map(lambda a: lax.all_gather(a, axis), part)  146 us
    psum x1, blocking collectives, shards(): pooled = lax.psum(partial_value, 'seq')  94.9 us
    all_gather x1, waiting for transfers between devices, shards(): lax.all_gather(rows_here[:, width:2 * width], 'seq', axis=0, tiled=True)  82.9 us
    all_gather x1, waiting for transfers between devices, shards(): lax.all_gather(rows_here[:, 2 * width:], 'seq', axis=0, tiled=True)  80.6 us
    all_gather x1, waiting for transfers between devices, shards(): lax.all_gather(rows_here[:, :width], 'seq', axis=0, tiled=True)  48.1 us
    all_gather x1, blocking collectives, carried_in(): gathered = jax.tree.map(lambda a: lax.all_gather(a, axis), part)  31.5 us
    ppermute x1, starting transfers between devices, partner_2(): return lax.ppermute(block, axis, route)  23.3 us
    all_gather x1, blocking collectives, shards(): group = lax.all_gather(full_vec, 'dp', axis=0, tiled=True)  20.9 us
  transfers between devices with their start and end apart: 5, of which 5 were waited for; matrix products, arithmetic and copies ran while one was open for 2% of the time, Pallas kernels for 0%

commit v1 on v0

--- a/solution.py
+++ b/solution.py
@@ -60,7 +60,14 @@
         return jnp.dot(normed, piece, preferred_element_type=jnp.float32)
 
     query_raw = add_rows(lax.all_gather(rows_here[:, :width], "seq", axis=0, tiled=True))
-    key_raw = add_rows(lax.all_gather(rows_here[:, width : 2 * width], "seq", axis=0, tiled=True))
+    key_raw = add_rows(
+        jnp.concatenate(
+            lax.all_to_all(
+                jnp.stack([rows_here[:, width : 2 * width]] * lax.axis_size("seq")), "seq", 0, 0
+            ),
+            axis=0,
+        )
+    )
     value_raw = add_rows(lax.all_gather(rows_here[:, 2 * width :], "seq", axis=0, tiled=True))
     positions = seq_place * tokens_dev + jnp.arange(tokens_dev)
     valid = positions[None, :] < lengths[0][:, None]

time: 568 us -> 490 us (0.86)
  waiting for transfers between devices: 359 us -> 272 us
  starting transfers between devices: 23.4 us -> 34 us
    all_gather x1 -> x0, waiting for transfers between devices: 82.9 us -> none  [shards(): lax.all_gather(rows_here[:, width:2 * width], 'seq', axis=0, tiled=True)]
    all_gather x1, waiting for transfers between devices: 80.6 us -> 26.8 us  [shards(): lax.all_gather(rows_here[:, 2 * width:], 'seq', axis=0, tiled=True)]
    all_to_all x0 -> x1, waiting for transfers between devices: none -> 50 us  [shards(): lax.all_to_all(jnp.stack([rows_here[:, width:2 * width]] * lax.axis_size(...]
    all_to_all x0 -> x1, starting transfers between devices: none -> 10.6 us  [shards(): lax.all_to_all(jnp.stack([rows_here[:, width:2 * width]] * lax.axis_size(...]
where the time goes in v1:
time: 490 us; the launch traced here: 489 us
  waiting for transfers between devices  272 us (56%)
  blocking collectives  147 us (30%)
  starting transfers between devices  34 us (7%)
  between operations  17.8 us (4%)
  matrix products  11.6 us (2%)
  local copies, waits for them, and re-layouts  4.97 us (1%)
    all_gather x1, waiting for transfers between devices, carried_in(): gathered = jax.tree.map(lambda a: lax.all_gather(a, axis), part)  146 us
    psum x1, blocking collectives, shards(): pooled = lax.psum(partial_value, 'seq')  94.8 us
    all_to_all x1, waiting for transfers between devices, shards(): lax.all_to_all(jnp.stack([rows_here[:, width:2 * width]] * lax.axis_size(...  50 us
    all_gather x1, waiting for transfers between devices, shards(): lax.all_gather(rows_here[:, :width], 'seq', axis=0, tiled=True)  48.2 us
    all_gather x1, blocking collectives, carried_in(): gathered = jax.tree.map(lambda a: lax.all_gather(a, axis), part)  31.7 us
    all_gather x1, waiting for transfers between devices, shards(): lax.all_gather(rows_here[:, 2 * width:], 'seq', axis=0, tiled=True)  26.8 us
    ppermute x1, starting transfers between devices, partner_2(): return lax.ppermute(block, axis, route)  23.3 us
    all_gather x1, blocking collectives, shards(): group = lax.all_gather(full_vec, 'dp', axis=0, tiled=True)  20.9 us
  transfers between devices with their start and end apart: 5, of which 5 were waited for; matrix products, arithmetic and copies ran while one was open for 2% of the time, Pallas kernels for 0%

profile of v1, /device:TPU:1, one launch (start us, length us, event | category | flops | bytes accessed | tf_op | source)
XLA Modules:
  0.0 488.6 jit_solution(4531365489495566197)
XLA Ops:
  7.2 0.0 all-gather.6.cloned.1.call-start
  7.2 1.6 fusion.56
  8.8 0.0 all-gather.6.cloned.1.call-update
  8.8 1.6 stack.2
  10.3 0.0 copy-start
  10.3 0.0 copy-start.2
  10.4 10.6 %all-to-all-start = ((bf16[32,32,1024]{2,1,0:T(8,128)(2,1)}), bf16[32,32,1024]{2,1,0:T(8,128)(2,1)S(1)}, u32[]{:S(2)}, u32[]{:S(2)}) async-start(bf16[32,32,1024]{2,1,0:T(8,128)(2,1)} %stack.2), calls=%async_computation | async-start | bytes 4194304 | tf_op jit(solution)/shard_map/all_to_all | solution.py:65
  21.0 0.0 all-gather.8.cloned.1.call-start
  21.0 0.7 all-gather.8.cloned.1.call-update
  21.7 0.0 all-gather.10.cloned.1.call-start
  22.4 0.0 copy-done
  22.5 0.2 fusion.5
  22.6 50.0 %all-to-all-done = bf16[32,32,1024]{2,1,0:T(8,128)(2,1)S(1)} async-done(((bf16[32,32,1024]{2,1,0:T(8,128)(2,1)}), bf16[32,32,1024]{2,1,0:T(8,128)(2,1)S(1)}, u32[]{:S(2)}, u32[]{:S(2)}) %all-to-all-start) | async-done | bytes 2097184 | tf_op jit(solution)/shard_map/all_to_all | solution.py:65
  72.7 0.0 copy-done.2
  72.7 1.2 convert_reduce_fusion
  73.9 0.2 copy.43
  74.1 0.0 copy-start.3
  74.1 26.8 %all-gather.6.cloned.1.call-done = bf16[1024,1024]{1,0:T(8,128)(2,1)} async-done(((bf16[32,1024]{1,0:T(8,128)(2,1)}), bf16[1024,1024]{1,0:T(8,128)(2,1)}) %all-gather.6.cloned.1.call-update) | async-done | bytes 2097168 | tf_op jit(solution)/shard_map/all_gather | solution.py:71
  100.9 2.3 fusion.3
  103.2 1.1 fusion.36
  104.3 0.0 all-gather.10.cloned.1.call-update
  104.4 0.0 copy-done.3
  104.4 0.7 dynamic_slice.15
  105.1 31.7 %all_gather.26 = f32[32,1,8,128]{3,2,1,0:T(8,128)S(1)} all-gather(f32[1,1,8,128]{3,2,1,0:T(8,128)S(1)} %bitcast.126), channel_id=1, replica_groups=mesh['seq'=32,'dp'=8,'domain'=2] {'seq'}, dimensions={0}, use_global_device_ids=true | all-gather | bytes 135168 | tf_op jit(solution)/shard_map/all_gather | solution.py:15
  136.7 48.2 %all-gather.8.cloned.1.call-done = bf16[1024,1024]{1,0:T(8,128)(2,1)} async-done(((bf16[32,1024]{1,0:T(8,128)(2,1)}), bf16[1024,1024]{1,0:T(8,128)(2,1)}) %all-gather.8.cloned.1.call-update) | async-done | bytes 2097168 | tf_op jit(solution)/shard_map/all_gather | solution.py:62
  184.9 2.7 fusion.24
  187.6 0.0 copy-start.4
  187.6 0.5 select_reduce_fusion
  188.2 0.4 fusion.13
  188.5 145.8 %all-gather.10.cloned.1.call-done = f32[256,128,128]{2,1,0:T(8,128)} async-done(((f32[8,128,128]{2,1,0:T(8,128)}), f32[256,128,128]{2,1,0:T(8,128)}) %all-gather.10.cloned.1.call-update) | async-done | bytes 16777232 | tf_op jit(solution)/shard_map/all_gather | solution.py:15
  334.4 0.0 copy-done.4
  334.4 0.5 fusion.31
  334.9 1.4 fusion.23
  336.4 0.0 copy-start.1
  336.4 0.3 copy.37
  336.7 0.2 fusion.7
  336.9 94.8 %psum.7 = f32[1,1024]{1,0:T(1,128)S(1)} all-reduce(f32[1,1024]{1,0:T(1,128)S(1)} %bitcast.123), channel_id=1, replica_groups=mesh['seq'=32,'dp'=8,'domain'=2] {'seq'}, use_global_device_ids=true, to_apply=%region_6.7 | all-reduce | flops 1024 | bytes 8192 | tf_op jit(solution)/shard_map/psum | solution.py:115
  431.7 0.6 multiply_reduce_fusion
  433.0 0.0 copy-done.1
  433.0 20.9 %all-gather.1 = bf16[8,1,1024]{2,1,0:T(2,128)(2,1)S(1)} all-gather(bf16[1,1,1024]{2,1,0:T(2,128)(2,1)S(1)} %bitcast.125), channel_id=1, replica_groups=mesh['seq'=32,'dp'=8,'domain'=2] {'dp'}, dimensions={0}, use_global_device_ids=true | all-gather | bytes 18432 | tf_op jit(solution)/shard_map/all_gather | solution.py:119
  453.9 23.3 %collective-permute-start = (bf16[8,1024]{1,0:T(8,128)(2,1)S(1)}, bf16[8,1024]{1,0:T(8,128)(2,1)S(1)}, u32[]{:S(2)}, u32[]{:S(2)}) collective-permute-start(bf16[8,1024]{1,0:T(8,128)(2,1)S(1)} %bitcast.124), channel_id=1, source_target_pairs={{0,1},{1,0},{2,3},{3,2},{4,5},{5,4},{6,7},{7,6},{8,9},{9,8},{10,11... | collective-permute-start | bytes 49160 | tf_op jit(solution)/shard_map/ppermute | solution.py:33
  477.2 0.6 dynamic-slice_bitcast_fusion
  477.8 0.2 collective-permute-done
  478.0 1.5 fusion.54
  (9 shorter events, 0.1 us)
Async XLA Ops:
  7.2 93.7 %all-gather.6.cloned.1.call-start = ((), (), s32[]{:S(2)}) async-start(), calls=%async_computation.1 | async-start | bytes 2162688 | tf_op jit(solution)/shard_map/all_gather | solution.py:71
  10.3 12.1 %copy-start = (bf16[1,1,256,1024]{3,2,1,0:T(8,128)(2,1)S(1)}, bf16[1,1,256,1024]{3,2,1,0:T(8,128)(2,1)}, u32[]{:S(2)}) copy-start(bf16[1,1,256,1024]{3,2,1,0:T(8,128)(2,1)} %param.8) | copy-start | bytes 1572868
  10.3 62.3 %copy-start.2 = (f32[1,1024]{1,0:T(1,128)S(1)}, f32[1,1024]{1,0:T(1,128)}, u32[]{:S(2)}) copy-start(f32[1,1024]{1,0:T(1,128)} %param.10) | copy-start | bytes 12292
  10.4 62.3 %all-to-all-start = ((bf16[32,32,1024]{2,1,0:T(8,128)(2,1)}), bf16[32,32,1024]{2,1,0:T(8,128)(2,1)S(1)}, u32[]{:S(2)}, u32[]{:S(2)}) async-start(bf16[32,32,1024]{2,1,0:T(8,128)(2,1)} %stack.2), calls=%async_computation | async-start | bytes 4194304 | tf_op jit(solution)/shard_map/all_to_all | solution.py:65
  21.0 163.9 %all-gather.8.cloned.1.call-start = ((), (), s32[]{:S(2)}) async-start(), calls=%async_computation.2 | async-start | bytes 2162688 | tf_op jit(solution)/shard_map/all_gather | solution.py:62
  21.7 312.6 %all-gather.10.cloned.1.call-start = ((), (), s32[]{:S(2)}) async-start(), calls=%async_computation.3 | async-start | bytes 17301504 | tf_op jit(solution)/shard_map/all_gather | solution.py:15
  74.1 30.3 %copy-start.3 = (s32[8]{0:T(128)S(1)}, s32[8]{0:T(128)}, u32[]{:S(2)}) copy-start(s32[8]{0:T(128)} %param.13) | copy-start | bytes 100
  187.6 146.8 %copy-start.4 = (bf16[32,8,8,128]{3,2,1,0:T(8,128)(2,1)}, bf16[32,8,8,128]{3,2,1,0:T(8,128)(2,1)S(1)}, u32[]{:S(2)}) copy-start(bf16[32,8,8,128]{3,2,1,0:T(8,128)(2,1)S(1)} %fusion.24) | copy-start | bytes 1572868
  336.4 96.7 %copy-start.1 = (f32[1,1024]{1,0:T(1,128)S(1)}, f32[1,1024]{1,0:T(1,128)}, u32[]{:S(2)}) copy-start(f32[1,1024]{1,0:T(1,128)} %param.11) | copy-start | bytes 12292
  453.9 24.1 %collective-permute-start = (bf16[8,1024]{1,0:T(8,128)(2,1)S(1)}, bf16[8,1024]{1,0:T(8,128)(2,1)S(1)}, u32[]{:S(2)}, u32[]{:S(2)}) collective-permute-start(bf16[8,1024]{1,0:T(8,128)(2,1)S(1)} %bitcast.124), channel_id=1, source_target_pairs={{0,1},{1,0},{2,3},{3,2},{4,5},{5,4},{6,7},{7,6},{8,9},{9,8},{10,11... | collective-permute-start | bytes 49160 | tf_op jit(solution)/shard_map/ppermute | solution.py:33
Sparse Core Ops, SparseCore 0:
  11.1 89.7 all-gather.5
  104.1 80.7 all-gather.7
  188.1 146.2 all-gather.9
